TPU v7x, 32 devices: a whole 2x2x4 slice. The times are simulated.
32 devices in a mesh: dp: 4 (over x, core), mp: 8 (over z, y).
Axes of the slice: x: 2, y: 2, z: 4, core: 2. Of those that a mesh axis runs over, the one named last changes fastest.
Arguments:
- block_input: bfloat16 [4096, 2048], P(('dp', 'mp')), may hold values from -6 to 6
- out_cotangent: bfloat16 [4096, 2048], P(('dp', 'mp')), may hold values from -6 to 6
- segments: int32 [4, 1024], P('dp'), may hold values from 0 to 3, never falling along the last dimension, each value on 1 to 512 neighbouring positions
- domain_tags: int32 [4], P('dp'), may hold values from 0 to 7
- counts: int32 [8], replicated, may hold values from 1 to 4
- attn_gain: float32 [2048], replicated, may hold values from 0.5 to 1.5
- mlp_gain: float32 [2048], replicated, may hold values from 0.5 to 1.5
- norm_gain: float32 [2048], P('mp'), may hold values from 0.5 to 1.5
- bound_table: float32 [24, 2048], P(None, 'mp'), may hold values from -4 to 4
- w_input: bfloat16 [2048, 2048], P(None, 'mp'), may hold values from -0.125 to 0.125
- w_forget: bfloat16 [2048, 2048], P(None, 'mp'), may hold values from -0.125 to 0.125
- w_gate_mix: bfloat16 [2048, 2048], P(None, 'mp'), may hold values from -0.125 to 0.125
- w_out: bfloat16 [2048, 2048], P('mp'), may hold values from -0.1875 to 0.1875
- w_glu_gate: bfloat16 [2048, 5632], P(None, 'mp'), may hold values from -0.125 to 0.125
- w_glu_up: bfloat16 [2048, 5632], P(None, 'mp'), may hold values from -0.125 to 0.125
- w_glu_down: bfloat16 [5632, 2048], P('mp'), may hold values from -0.109375 to 0.109375
Outputs:
- result: bfloat16 [4096, 2048], P(('dp', 'mp'))
- grad_block_input: float32 [4096, 2048], P(('dp', 'mp'))
- grad_attn_gain: float32 [2048], replicated
- grad_mlp_gain: float32 [2048], replicated
- grad_norm_gain: float32 [2048], replicated
- grad_bound_table: float32 [24, 2048], replicated
- grad_input: float32 [2048, 2048], P('dp', 'mp')
- grad_forget: float32 [2048, 2048], P('dp', 'mp')
- grad_gate_mix: float32 [2048, 2048], P('dp', 'mp')
- grad_out: float32 [2048, 2048], P('mp', 'dp')
- grad_glu_gate: float32 [2048, 5632], P('dp', 'mp')
- grad_glu_up: float32 [2048, 5632], P('dp', 'mp')
- grad_glu_down: float32 [5632, 2048], P('mp', 'dp')
Inputs may be any that keep to these rules, and one draw needn't show every extreme that they name: `segments`: along each row the document ids never fall; each document has at least one position.
All inputs are finite; a program needn't handle non-finite values.
Results may differ from a plain program's by a relative error of at most 0.022.
Values may be sent and summed in bfloat16 or wider, within the bound.
No kernel may reach another device: no remote copies, remote signals or barrier semaphores. Data moves between devices by JAX's collectives and lax.ppermute only.
A program may use at most 320 MiB of HBM per device.

v0:
```python
import jax
import jax.numpy as jnp
from jax import lax
from jax.sharding import PartitionSpec as P

NLAYER = 24
LAYER = 20
LEN = 1024
BLK = 128
NDOM = 8
EPS = 1e-06
HIGH = lax.Precision.HIGHEST


def inverse_rms(rows):
    return lax.rsqrt(jnp.mean(rows * rows, axis=1, keepdims=True) + EPS)


def silu_slope(value):
    sig = jax.nn.sigmoid(value)
    return sig * (1.0 + value * (1.0 - sig))


def norm_back(grad_normed, rows, inverse, gain):
    scaled = grad_normed * gain
    unit = rows * inverse
    back = inverse * (scaled - unit * jnp.mean(scaled * unit, axis=1, keepdims=True))
    return (back, jnp.sum(grad_normed * unit, axis=0))


def block_terms(log_blk, reset_blk, lower):
    cum_log = jnp.einsum("csu,tu->cst", log_blk, lower, precision=HIGH)
    cum_reset = jnp.einsum("su,tu->st", reset_blk, lower, precision=HIGH)
    same = (cum_reset[:, :, None] == cum_reset[:, None, :]) & (lower[None] > 0.5)
    spread = jnp.minimum(cum_log[:, :, :, None] - cum_log[:, :, None, :], 0.0)
    weight = jnp.where(same[None], jnp.exp(spread), 0.0)
    return (weight, cum_log, cum_reset)


def local(
    block_input,
    out_cotangent,
    segments,
    domain_tags,
    counts,
    attn_gain,
    mlp_gain,
    norm_gain,
    bound_table,
    w_input,
    w_forget,
    w_gate_mix,
    w_out,
    w_glu_gate,
    w_glu_up,
    w_glu_down,
):
    rows_dev, width = block_input.shape
    chans = w_input.shape[1]
    units = w_glu_gate.shape[1]
    seqs = segments.shape[0]
    total_rows = seqs * LEN
    nblk = LEN // BLK
    mp_index = lax.axis_index("mp")
    own_start = mp_index * rows_dev
    own_rows = block_input.astype(jnp.float32)
    own_inv1 = inverse_rms(own_rows)
    input_all = lax.all_gather(block_input, "mp", axis=0, tiled=True)
    input_all_f = input_all.astype(jnp.float32)
    normed_all = (input_all_f * inverse_rms(input_all_f) * attn_gain).astype(jnp.bfloat16)
    w_mix = jnp.concatenate([w_input, w_forget, w_gate_mix], axis=1)
    pre_mix = jnp.einsum("td,dc->ct", normed_all, w_mix, preferred_element_type=jnp.float32)
    pre_i = pre_mix[:chans].reshape(chans, seqs, LEN)
    pre_f = pre_mix[chans : 2 * chans].reshape(chans, seqs, LEN)
    pre_g = pre_mix[2 * chans :]
    shares = jax.nn.softmax(bound_table, axis=0)
    layer_ids = jnp.arange(NLAYER)
    pick = ((layer_ids >= 1) & (layer_ids <= LAYER)).astype(jnp.float32)[:, None]
    bound_vec = jnp.sum(shares * pick, axis=0)
    bound = bound_vec[:, None, None]
    sig_f = jax.nn.sigmoid(pre_f)
    forget = bound + (1.0 - bound) * sig_f
    act_i = jax.nn.silu(pre_i)
    update = act_i * (1.0 - forget)
    keep = jnp.concatenate(
        [
            jnp.zeros((seqs, 1), jnp.float32),
            (segments[:, 1:] == segments[:, :-1]).astype(jnp.float32),
        ],
        axis=1,
    )
    positions = jnp.arange(BLK)
    lower = (positions[None, :] <= positions[:, None]).astype(jnp.float32)

    def split_blocks(arr):
        arr = arr.reshape(arr.shape[:-1] + (nblk, BLK))
        return jnp.moveaxis(arr, -2, 0)

    def join_blocks(arr):
        arr = jnp.moveaxis(arr, 0, -2)
        return arr.reshape(arr.shape[:-2] + (LEN,))

    log_blocks = split_blocks(jnp.log(forget))
    reset_blocks = split_blocks(1.0 - keep)

    def forward_step(state, blk):
        log_blk, reset_blk, update_blk = blk
        weight, cum_log, cum_reset = block_terms(log_blk, reset_blk, lower)
        lead = jnp.where(cum_reset[None] == 0.0, jnp.exp(cum_log), 0.0)
        states_blk = (
            jnp.einsum("cstu,csu->cst", weight, update_blk, precision=HIGH)
            + lead * state[:, :, None]
        )
        return (states_blk[:, :, -1], states_blk)

    _, state_blocks = lax.scan(
        forward_step,
        jnp.zeros((chans, seqs), jnp.float32),
        (log_blocks, reset_blocks, split_blocks(update)),
    )
    states3 = join_blocks(state_blocks)
    states = states3.reshape(chans, total_rows)
    square_sum = lax.psum(jnp.sum(states * states, axis=0), "mp")
    rec_inv = lax.rsqrt(square_sum / width + EPS)
    unit_states = states * rec_inv[None, :]
    act_g = jax.nn.silu(pre_g)
    gated = (unit_states * norm_gain[:, None] * act_g).astype(jnp.bfloat16)
    partial_mix = jnp.einsum("ct,cd->td", gated, w_out, preferred_element_type=jnp.float32)
    middle_all = input_all_f + lax.psum(partial_mix.astype(jnp.bfloat16), "mp").astype(jnp.float32)
    normed_two_all = (middle_all * inverse_rms(middle_all) * mlp_gain).astype(jnp.bfloat16)
    middle = lax.dynamic_slice_in_dim(middle_all, own_start, rows_dev, 0)
    own_inv2 = inverse_rms(middle)
    w_glu = jnp.concatenate([w_glu_gate, w_glu_up], axis=1)
    gate_up = jnp.dot(normed_two_all, w_glu, preferred_element_type=jnp.float32)
    gate = gate_up[:, :units]
    up = gate_up[:, units:]
    act_gate = jax.nn.silu(gate)
    hidden = (act_gate * up).astype(jnp.bfloat16)
    piece = hidden
    final = middle + lax.psum_scatter(
        jnp.dot(piece, w_glu_down, preferred_element_type=jnp.float32).astype(jnp.bfloat16),
        "mp",
        scatter_dimension=0,
        tiled=True,
    ).astype(jnp.float32)
    result = final.astype(jnp.bfloat16)
    domain_hit = (domain_tags[:, None] == jnp.arange(NDOM)[None, :]).astype(jnp.float32)
    seq_count = jnp.dot(domain_hit, counts.astype(jnp.float32)[:, None], precision=HIGH)[:, 0]
    seq_weight = lax.rsqrt(seq_count)
    cot_all = lax.all_gather(out_cotangent, "mp", axis=0, tiled=True)
    grad_all = (
        cot_all.astype(jnp.float32).reshape(seqs, LEN, width) * seq_weight[:, None, None]
    ).reshape(total_rows, width)
    grad_all_b = grad_all.astype(jnp.bfloat16)
    grad_own = lax.dynamic_slice_in_dim(grad_all, own_start, rows_dev, 0)
    grad_hidden = jnp.einsum(
        "td,fd->tf", grad_all_b, w_glu_down, preferred_element_type=jnp.float32
    )
    down_term = jnp.einsum("tf,td->fd", hidden, grad_all_b, preferred_element_type=jnp.float32)
    grad_gate = grad_hidden * up * silu_slope(gate)
    grad_up = grad_hidden * act_gate
    grad_gate_up = jnp.concatenate([grad_gate, grad_up], axis=1).astype(jnp.bfloat16)
    piece = grad_gate_up
    grad_normed_two = lax.psum_scatter(
        jnp.einsum("tf,df->td", piece, w_glu, preferred_element_type=jnp.float32).astype(
            jnp.bfloat16
        ),
        "mp",
        scatter_dimension=0,
        tiled=True,
    ).astype(jnp.float32)
    back_two, mlp_gain_term = norm_back(grad_normed_two, middle, own_inv2, mlp_gain)
    grad_middle = grad_own + back_two
    middle_grad_all = lax.all_gather(grad_middle.astype(jnp.bfloat16), "mp", axis=0, tiled=True)
    grad_gated = jnp.einsum("td,cd->ct", middle_grad_all, w_out, preferred_element_type=jnp.float32)
    out_term = jnp.einsum("ct,td->cd", gated, middle_grad_all, preferred_element_type=jnp.float32)
    grad_unit = grad_gated * norm_gain[:, None] * act_g
    norm_gain_term = jnp.sum(grad_gated * unit_states * act_g, axis=1)
    grad_pre_g = grad_gated * unit_states * norm_gain[:, None] * silu_slope(pre_g)
    inner = lax.psum(jnp.sum(grad_unit * unit_states, axis=0), "mp")
    grad_states = rec_inv[None, :] * (grad_unit - unit_states * (inner / width)[None, :])
    forget_heads = split_blocks(forget)[..., 0]
    keep_heads = split_blocks(keep)[..., 0]

    def backward_step(carry, blk):
        log_blk, reset_blk, grad_blk, forget_head, keep_head = blk
        weight, cum_log, cum_reset = block_terms(log_blk, reset_blk, lower)
        trailing = jnp.where(
            (cum_reset == cum_reset[:, -1:])[None], jnp.exp(cum_log[:, :, -1:] - cum_log), 0.0
        )
        total = (
            jnp.einsum("cstu,cst->csu", weight, grad_blk, precision=HIGH)
            + trailing * carry[:, :, None]
        )
        return (forget_head * keep_head[None] * total[:, :, 0], total)

    _, grad_blocks = lax.scan(
        backward_step,
        jnp.zeros((chans, seqs), jnp.float32),
        (
            log_blocks,
            reset_blocks,
            split_blocks(grad_states.reshape(chans, seqs, LEN)),
            forget_heads,
            keep_heads,
        ),
        reverse=True,
    )
    grad_update = join_blocks(grad_blocks)
    prior = jnp.concatenate([jnp.zeros((chans, seqs, 1), jnp.float32), states3[:, :, :-1]], axis=2)
    grad_forget = grad_update * keep[None] * prior - grad_update * act_i
    grad_pre_i = grad_update * (1.0 - forget) * silu_slope(pre_i)
    grad_pre_f = grad_forget * (1.0 - bound) * sig_f * (1.0 - sig_f)
    bound_grad = jnp.sum(grad_forget * (1.0 - sig_f), axis=(1, 2))
    pick_grad = pick * bound_grad[None, :]
    table_term = shares * (pick_grad - jnp.sum(shares * pick_grad, axis=0, keepdims=True))
    grad_pre = jnp.concatenate(
        [grad_pre_i.reshape(chans, total_rows), grad_pre_f.reshape(chans, total_rows), grad_pre_g],
        axis=0,
    ).astype(jnp.bfloat16)
    piece = grad_pre
    grad_normed = lax.psum_scatter(
        jnp.einsum("ct,dc->td", piece, w_mix, preferred_element_type=jnp.float32).astype(
            jnp.bfloat16
        ),
        "mp",
        scatter_dimension=0,
        tiled=True,
    ).astype(jnp.float32)
    back_one, attn_gain_term = norm_back(grad_normed, own_rows, own_inv1, attn_gain)
    grad_block_input = grad_middle + back_one
    mix_part = jnp.einsum("tk,ct->kc", normed_all, grad_pre, preferred_element_type=jnp.float32)
    glu_part = jnp.einsum(
        "tk,tf->kf", normed_two_all, grad_gate_up, preferred_element_type=jnp.float32
    )
    weight_grads = lax.psum_scatter(
        jnp.concatenate([mix_part, glu_part], axis=1).astype(jnp.bfloat16),
        "dp",
        scatter_dimension=0,
        tiled=True,
    ).astype(jnp.float32)
    out_grad, down_grad = (
        lax.psum_scatter(
            out_term.astype(jnp.bfloat16), "dp", scatter_dimension=1, tiled=True
        ).astype(jnp.float32),
        lax.psum_scatter(
            down_term.astype(jnp.bfloat16), "dp", scatter_dimension=1, tiled=True
        ).astype(jnp.float32),
    )
    groups = lax.axis_size("mp")
    onehot = (jnp.arange(groups) == mp_index).astype(jnp.float32)
    norm_full = (onehot[:, None] * norm_gain_term[None, :]).reshape(width)
    table_full = (table_term[:, None, :] * onehot[None, :, None]).reshape(NLAYER, width)
    attn_sum, mlp_sum, norm_sum, table_sum = lax.psum(
        (attn_gain_term, mlp_gain_term, norm_full, table_full), ("dp", "mp")
    )
    grad_input = weight_grads[:, :chans]
    grad_forget_w = weight_grads[:, chans : 2 * chans]
    grad_gate_mix = weight_grads[:, 2 * chans : 3 * chans]
    grad_glu_gate = weight_grads[:, 3 * chans : 3 * chans + units]
    grad_glu_up = weight_grads[:, 3 * chans + units :]
    return (
        result,
        grad_block_input,
        attn_sum,
        mlp_sum,
        norm_sum,
        table_sum,
        grad_input,
        grad_forget_w,
        grad_gate_mix,
        out_grad,
        grad_glu_gate,
        grad_glu_up,
        down_grad,
    )


def solution(mesh):
    placed = (
        P(("dp", "mp"), None),
        P(("dp", "mp"), None),
        P("dp", None),
        P("dp"),
        P(),
        P(),
        P(),
        P("mp"),
        P(None, "mp"),
        P(None, "mp"),
        P(None, "mp"),
        P(None, "mp"),
        P("mp", None),
        P(None, "mp"),
        P(None, "mp"),
        P("mp", None),
    )
    return jax.shard_map(
        local,
        mesh=mesh,
        in_specs=placed,
        out_specs=(
            P(("dp", "mp"), None),
            P(("dp", "mp"), None),
            P(),
            P(),
            P(),
            P(),
            P("dp", "mp"),
            P("dp", "mp"),
            P("dp", "mp"),
            P("mp", "dp"),
            P("dp", "mp"),
            P("dp", "mp"),
            P("mp", "dp"),
        ),
        check_vma=False,
    )
```

profile of v0, /device:TPU:10, one launch (start us, length us, event | category | flops | bytes accessed | tf_op | source)
XLA Modules:
  0.0 1434.1 jit_solution(5197083218827090929)
XLA Ops:
  17.3 66.8 %all-gather.4.cloned.1.call-done = bf16[1024,2048]{1,0:T(8,128)(2,1)} async-done(((bf16[128,2048]{1,0:T(8,128)(2,1)}), bf16[1024,2048]{1,0:T(8,128)(2,1)}) %all-gather.4.cloned.1.call-update) | async-done | bytes 4194320 | tf_op jit(solution)/shard_map/all_gather | solution.py:68
  100.1 259.9 %while.32 = (s32[]{:T(128)}, f32[256,1]{0,1:T(1,128)S(1)}, f32[8,256,1,128]{1,3,2,0:T(8,128)}, f32[8,1,128]{2,1,0:T(1,128)S(1)}, f32[8,256,1,128]{3,2,1,0:T(1,128)}, /*index=5*/f32[8,256,1,128]{3,2,1,0:T(1,128)}, s32[]{:T(128)}) while((s32[]{:T(128)}, f32[256,1]{0,1:T(1,128)S(1)}, f32[8,256,1,128]{1,3,2,0:T(8,128)}, ...), condition=%wide.region_5.6_spmd.clone.clone, body=%wide.region_4.0_spmd.clone.clone.sunk | while | flops 113787008 | bytes 2398181 | solution.py:116
  102.0 28.5 %fusion.137 = f32[256,1,128]{2,1,0:T(1,128)S(1)} fusion(f32[256,128]{1,0:T(8,128)S(1)} %copy.93, pred[128,128]{1,0:T(8,128)(4,1)S(1)} %fusion.136, f32[8,256,1,128]{3,2,1,0:T(1,128)} %get-tuple-element.526, s32[]{:T(128)S(6)} %copy.104), kind=kOutput, calls=%fused_computation.2.clone.1 | convolution fusion | flops 62914560 | bytes 540676 | tf_op jit(solution)/shard_map/while/body/eval_jaxpr/cstu,csu->cst/dot_general | solution.py:111
  133.1 28.5 %fusion.137 = f32[256,1,128]{2,1,0:T(1,128)S(1)} fusion(f32[256,128]{1,0:T(8,128)S(1)} %copy.93, pred[128,128]{1,0:T(8,128)(4,1)S(1)} %fusion.136, f32[8,256,1,128]{3,2,1,0:T(1,128)} %get-tuple-element.526, s32[]{:T(128)S(6)} %copy.104), kind=kOutput, calls=%fused_computation.2.clone.1 | convolution fusion | flops 62914560 | bytes 540676 | tf_op jit(solution)/shard_map/while/body/eval_jaxpr/cstu,csu->cst/dot_general | solution.py:111
  164.3 28.5 %fusion.137 = f32[256,1,128]{2,1,0:T(1,128)S(1)} fusion(f32[256,128]{1,0:T(8,128)S(1)} %copy.93, pred[128,128]{1,0:T(8,128)(4,1)S(1)} %fusion.136, f32[8,256,1,128]{3,2,1,0:T(1,128)} %get-tuple-element.526, s32[]{:T(128)S(6)} %copy.104), kind=kOutput, calls=%fused_computation.2.clone.1 | convolution fusion | flops 62914560 | bytes 540676 | tf_op jit(solution)/shard_map/while/body/eval_jaxpr/cstu,csu->cst/dot_general | solution.py:111
  195.4 28.5 %fusion.137 = f32[256,1,128]{2,1,0:T(1,128)S(1)} fusion(f32[256,128]{1,0:T(8,128)S(1)} %copy.93, pred[128,128]{1,0:T(8,128)(4,1)S(1)} %fusion.136, f32[8,256,1,128]{3,2,1,0:T(1,128)} %get-tuple-element.526, s32[]{:T(128)S(6)} %copy.104), kind=kOutput, calls=%fused_computation.2.clone.1 | convolution fusion | flops 62914560 | bytes 540676 | tf_op jit(solution)/shard_map/while/body/eval_jaxpr/cstu,csu->cst/dot_general | solution.py:111
  226.6 28.5 %fusion.137 = f32[256,1,128]{2,1,0:T(1,128)S(1)} fusion(f32[256,128]{1,0:T(8,128)S(1)} %copy.93, pred[128,128]{1,0:T(8,128)(4,1)S(1)} %fusion.136, f32[8,256,1,128]{3,2,1,0:T(1,128)} %get-tuple-element.526, s32[]{:T(128)S(6)} %copy.104), kind=kOutput, calls=%fused_computation.2.clone.1 | convolution fusion | flops 62914560 | bytes 540676 | tf_op jit(solution)/shard_map/while/body/eval_jaxpr/cstu,csu->cst/dot_general | solution.py:111
  257.7 28.5 %fusion.137 = f32[256,1,128]{2,1,0:T(1,128)S(1)} fusion(f32[256,128]{1,0:T(8,128)S(1)} %copy.93, pred[128,128]{1,0:T(8,128)(4,1)S(1)} %fusion.136, f32[8,256,1,128]{3,2,1,0:T(1,128)} %get-tuple-element.526, s32[]{:T(128)S(6)} %copy.104), kind=kOutput, calls=%fused_computation.2.clone.1 | convolution fusion | flops 62914560 | bytes 540676 | tf_op jit(solution)/shard_map/while/body/eval_jaxpr/cstu,csu->cst/dot_general | solution.py:111
  288.9 28.5 %fusion.137 = f32[256,1,128]{2,1,0:T(1,128)S(1)} fusion(f32[256,128]{1,0:T(8,128)S(1)} %copy.93, pred[128,128]{1,0:T(8,128)(4,1)S(1)} %fusion.136, f32[8,256,1,128]{3,2,1,0:T(1,128)} %get-tuple-element.526, s32[]{:T(128)S(6)} %copy.104), kind=kOutput, calls=%fused_computation.2.clone.1 | convolution fusion | flops 62914560 | bytes 540676 | tf_op jit(solution)/shard_map/while/body/eval_jaxpr/cstu,csu->cst/dot_general | solution.py:111
  320.0 28.5 %fusion.137 = f32[256,1,128]{2,1,0:T(1,128)S(1)} fusion(f32[256,128]{1,0:T(8,128)S(1)} %copy.93, pred[128,128]{1,0:T(8,128)(4,1)S(1)} %fusion.136, f32[8,256,1,128]{3,2,1,0:T(1,128)} %get-tuple-element.526, s32[]{:T(128)S(6)} %copy.104), kind=kOutput, calls=%fused_computation.2.clone.1 | convolution fusion | flops 62914560 | bytes 540676 | tf_op jit(solution)/shard_map/while/body/eval_jaxpr/cstu,csu->cst/dot_general | solution.py:111
  395.8 145.9 %all-reduce.5.cloned.1.call-done = bf16[1024,2048]{1,0:T(8,128)(2,1)} async-done(((bf16[1024,2048]{1,0:T(8,128)(2,1)}), bf16[1024,2048]{1,0:T(8,128)(2,1)}) %all-reduce.5.cloned.1.call-update) | async-done | bytes 4194320 | tf_op jit(solution)/shard_map/psum | solution.py:129
  561.3 56.1 %all-gather.6.cloned.1.call-done = bf16[1024,2048]{1,0:T(8,128)(2,1)} async-done(((bf16[128,2048]{1,0:T(8,128)(2,1)}), bf16[1024,2048]{1,0:T(8,128)(2,1)}) %all-gather.6.cloned.1.call-update) | async-done | bytes 4194320 | tf_op jit(solution)/shard_map/all_gather | solution.py:150
  647.5 79.2 %reduce-scatter.9.cloned.1.call-done = bf16[128,2048]{1,0:T(8,128)(2,1)} async-done(((bf16[1024,2048]{1,0:T(8,128)(2,1)}), bf16[128,2048]{1,0:T(8,128)(2,1)}) %reduce-scatter.9.cloned.1.call-update) | async-done | bytes 524304 | tf_op jit(solution)/shard_map/reduce_scatter | solution.py:164
  747.4 56.4 %all-gather.8.cloned.1.call-done = bf16[1024,2048]{1,0:T(8,128)(2,1)} async-done(((bf16[128,2048]{1,0:T(8,128)(2,1)}), bf16[1024,2048]{1,0:T(8,128)(2,1)}) %all-gather.8.cloned.1.call-update) | async-done | bytes 4194320 | tf_op jit(solution)/shard_map/all_gather | solution.py:174
  835.1 182.9 %while.33 = (s32[]{:T(128)}, f32[256,1]{0,1:T(1,128)S(1)}, f32[8,256,1,128]{1,3,2,0:T(8,128)}, f32[8,256,1]{1,2,0:T(1,128)S(1)}, f32[8,1]{0,1:T(1,128)S(1)}, /*i...) while((s32[]{:T(128)}, f32[256,1]{0,1:T(1,128)S(1)}, ...), condition=%wide.region_18.19_spmd.clone.clone, body=%wide.region_17.18_spmd.clone.clone.sunk | while | flops 113853312 | bytes 2405947 | solution.py:197
  838.1 17.7 %fusion.148 = f32[256,1,128]{2,1,0:T(1,128)S(1)} fusion(f32[256,128]{1,0:T(8,128)S(1)} %copy.95, pred[128,128]{1,0:T(8,128)(4,1)S(1)} %fusion.147, f32[8,256,1,128]{3,2,1,0:T(1,128)} %get-tuple-element.557, s32[]{:T(128)S(6)} %sub.280), kind=kOutput, calls=%fused_computation.30.clone.1 | convolution fusion | flops 62914560 | bytes 540676 | tf_op jit(solution)/shard_map/while/body/eval_jaxpr/cstu,cst->csu/dot_general | solution.py:192
  861.0 17.7 %fusion.148 = f32[256,1,128]{2,1,0:T(1,128)S(1)} fusion(f32[256,128]{1,0:T(8,128)S(1)} %copy.95, pred[128,128]{1,0:T(8,128)(4,1)S(1)} %fusion.147, f32[8,256,1,128]{3,2,1,0:T(1,128)} %get-tuple-element.557, s32[]{:T(128)S(6)} %sub.280), kind=kOutput, calls=%fused_computation.30.clone.1 | convolution fusion | flops 62914560 | bytes 540676 | tf_op jit(solution)/shard_map/while/body/eval_jaxpr/cstu,cst->csu/dot_general | solution.py:192
  929.4 17.7 %fusion.148 = f32[256,1,128]{2,1,0:T(1,128)S(1)} fusion(f32[256,128]{1,0:T(8,128)S(1)} %copy.95, pred[128,128]{1,0:T(8,128)(4,1)S(1)} %fusion.147, f32[8,256,1,128]{3,2,1,0:T(1,128)} %get-tuple-element.557, s32[]{:T(128)S(6)} %sub.280), kind=kOutput, calls=%fused_computation.30.clone.1 | convolution fusion | flops 62914560 | bytes 540676 | tf_op jit(solution)/shard_map/while/body/eval_jaxpr/cstu,cst->csu/dot_general | solution.py:192
  997.9 17.7 %fusion.148 = f32[256,1,128]{2,1,0:T(1,128)S(1)} fusion(f32[256,128]{1,0:T(8,128)S(1)} %copy.95, pred[128,128]{1,0:T(8,128)(4,1)S(1)} %fusion.147, f32[8,256,1,128]{3,2,1,0:T(1,128)} %get-tuple-element.557, s32[]{:T(128)S(6)} %sub.280), kind=kOutput, calls=%fused_computation.30.clone.1 | convolution fusion | flops 62914560 | bytes 540676 | tf_op jit(solution)/shard_map/while/body/eval_jaxpr/cstu,cst->csu/dot_general | solution.py:192
  1077.6 46.3 %reduce-scatter.11.cloned.1.call-done = bf16[128,2048]{1,0:T(8,128)(2,1)} async-done(((bf16[1024,2048]{1,0:T(8,128)(2,1)}), bf16[128,2048]{1,0:T(8,128)(2,1)}) %reduce-scatter.11.cloned.1.call-update) | async-done | bytes 524304 | tf_op jit(solution)/shard_map/reduce_scatter | solution.py:222
  1125.4 42.5 %all-reduce.1 = (f32[2048]{0:T(1024)}, f32[2048]{0:T(1024)}, f32[2048]{0:T(1024)}) all-reduce(f32[2048]{0:T(1024)S(1)} %get-tuple-element.358, f32[2048]{0:T(1024)S(1)} %get-tuple-element.354, f32[2048]{0:T(1024)S(1)} %mul.516), channel_id=1, replica_groups=mesh['dp'=4,'mp'=8] {'dp','mp'}, use_global_device_ids=true, to_apply=%region_22.23 | all-reduce | flops 6144 | bytes 49152 | tf_op jit(solution)/shard_map/psum | solution.py:254
  1167.8 48.6 %reduce-scatter.7.cloned.1.call-done = bf16[128,2048]{1,0:T(8,128)(2,1)} async-done(((bf16[1024,2048]{1,0:T(8,128)(2,1)}), bf16[128,2048]{1,0:T(8,128)(2,1)}) %reduce-scatter.7.cloned.1.call-update) | async-done | bytes 524304 | tf_op jit(solution)/shard_map/reduce_scatter | solution.py:140
  1220.1 72.7 %reduce-scatter.13.cloned.1.call-done = bf16[512,2176]{0,1:T(8,128)(2,1)} async-done(((bf16[2048,2176]{0,1:T(8,128)(2,1)}), bf16[512,2176]{0,1:T(8,128)(2,1)}) %reduce-scatter.13.cloned.1.call-update) | async-done | bytes 2228240 | tf_op jit(solution)/shard_map/reduce_scatter | solution.py:236
  1302.5 123.1 %all-reduce.7.cloned.1.call-done = f32[24,2048]{1,0:T(8,128)} async-done(((f32[24,2048]{1,0:T(8,128)}), f32[24,2048]{1,0:T(8,128)}) %all-reduce.7.cloned.1.call-update) | async-done | bytes 196624 | tf_op jit(solution)/shard_map/psum | solution.py:254
  (374 shorter events, 369.1 us)
Async XLA Ops:
  7.2 610.2 %copy-start = (bf16[704,2048]{1,0:T(8,128)(2,1)S(1)}, bf16[704,2048]{1,0:T(8,128)(2,1)}, u32[]{:S(2)}) copy-start(bf16[704,2048]{1,0:T(8,128)(2,1)} %param.35) | copy-start | bytes 8650756
  7.2 76.9 %all-gather.4.cloned.1.call-start = ((), (), s32[]{:S(2)}) async-start(), calls=%async_computation.6 | async-start | bytes 4718592 | tf_op jit(solution)/shard_map/all_gather | solution.py:68
  7.9 533.8 %all-reduce.5.cloned.1.call-start = ((), (), s32[]{:S(2)}) async-start(), calls=%async_computation.7 | async-start | bytes 8388608 | tf_op jit(solution)/shard_map/psum | solution.py:129
  11.4 81.7 %copy-start.24 = (f32[256]{0:T(256)}, f32[256]{0:T(256)S(1)}, u32[]{:S(2)}) copy-start(f32[256]{0:T(256)S(1)} %multiply_reduce_fusion.4) | copy-start | bytes 3076
  11.4 81.7 %copy-start.22 = (f32[256]{0:T(256)}, f32[256]{0:T(256)S(1)}, u32[]{:S(2)}) copy-start(f32[256]{0:T(256)S(1)} %broadcast_subtract_fusion.1) | copy-start | bytes 3076
  13.8 73.5 %copy-start.18 = (f32[2048]{0:T(1024)S(1)}, f32[2048]{0:T(1024)}, u32[]{:S(2)}) copy-start(f32[2048]{0:T(1024)} %param.25) | copy-start | bytes 24580
  100.1 280.5 %copy-start.32 = (f32[256]{0:T(256)S(1)}, f32[256]{0:T(256)}, u32[]{:S(2)}) copy-start(f32[256]{0:T(256)} %param.27) | copy-start | bytes 3076
  387.1 230.3 %all-gather.6.cloned.1.call-start = ((), (), s32[]{:S(2)}) async-start(), calls=%async_computation.9 | async-start | bytes 4718592 | tf_op jit(solution)/shard_map/all_gather | solution.py:150
  387.8 338.9 %reduce-scatter.9.cloned.1.call-start = ((), (), s32[]{:S(2)}) async-start(), calls=%async_computation.10 | async-start | bytes 4718592 | tf_op jit(solution)/shard_map/reduce_scatter | solution.py:164
  395.8 154.1 %copy-start.17 = (f32[2048]{0:T(1024)S(1)}, f32[2048]{0:T(1024)}, u32[]{:S(2)}) copy-start(f32[2048]{0:T(1024)} %param.26) | copy-start | bytes 24580
  541.7 8.2 copy-start.4
  541.7 8.2 copy-start.9
  639.4 164.4 %all-gather.8.cloned.1.call-start = ((), (), s32[]{:S(2)}) async-start(), calls=%async_computation.11 | async-start | bytes 4718592 | tf_op jit(solution)/shard_map/all_gather | solution.py:174
  731.4 340.9 %reduce-scatter.17.cloned.1.call-start = ((), (), s32[]{:S(2)}) async-start(), calls=%async_computation.16 | async-start | bytes 3604480 | tf_op jit(solution)/shard_map/reduce_scatter | solution.py:246
  739.3 336.5 %reduce-scatter.15.cloned.1.call-start = ((), (), s32[]{:S(2)}) async-start(), calls=%async_computation.15 | async-start | bytes 1310720 | tf_op jit(solution)/shard_map/reduce_scatter | solution.py:243
  834.0 289.9 %reduce-scatter.11.cloned.1.call-start = ((), (), s32[]{:S(2)}) async-start(), calls=%async_computation.12 | async-start | bytes 4718592 | tf_op jit(solution)/shard_map/reduce_scatter | solution.py:222
  1035.5 180.9 %reduce-scatter.7.cloned.1.call-start = ((), (), s32[]{:S(2)}) async-start(), calls=%async_computation.8 | async-start | bytes 4718592 | tf_op jit(solution)/shard_map/reduce_scatter | solution.py:140
  1042.0 13.6 copy-start.19
  1042.1 13.6 copy-start.31
  1042.1 250.7 %reduce-scatter.13.cloned.1.call-start = ((), (), s32[]{:S(2)}) async-start(), calls=%async_computation.14 | async-start | bytes 11141120 | tf_op jit(solution)/shard_map/reduce_scatter | solution.py:236
  1042.1 13.6 copy-start.5
  1042.1 13.6 copy-start.14
  1042.1 13.6 copy-start.16
  1071.1 354.5 %all-reduce.7.cloned.1.call-start = ((), (), s32[]{:S(2)}) async-start(), calls=%async_computation.13 | async-start | bytes 393216 | tf_op jit(solution)/shard_map/psum | solution.py:254
  (24 other events, 77.7 us)
Sparse Core Ops, SparseCore 0:
  10.2 73.8 all-gather.3
  387.2 154.4 all-reduce.4
  543.8 73.4 all-gather.5
  639.5 87.1 reduce-scatter.8
  731.5 72.2 all-gather.7
  806.3 34.3 reduce-scatter.16
  843.2 24.8 reduce-scatter.14
  1035.7 88.1 reduce-scatter.10
  1127.5 88.8 reduce-scatter.6
  1219.0 73.6 reduce-scatter.12
  1299.8 125.7 all-reduce.6
where the time goes:
time: 1440 us; the launch traced here: 1430 us
  waiting for transfers between devices  697 us (48%)
  matrix products  468 us (32%)
  other arithmetic  86.1 us (6%)
  local copies, waits for them, and re-layouts  78.9 us (5%)
  blocking collectives  75.7 us (5%)
  between operations  16.1 us (1%)
    dot_general x8, matrix products, forward_step(): jnp.einsum('cstu,csu->cst', weight, update_blk, precision=HIGH)  228 us
    psum x1, waiting for transfers between devices, local(): lax.psum(partial_mix.astype(jnp.bfloat16), 'mp').astype(jnp.float32)  146 us
    dot_general x8, matrix products, backward_step(): jnp.einsum('cstu,cst->csu', weight, grad_blk, precision=HIGH)  142 us
    psum x1, waiting for transfers between devices, local(): lax.psum((attn_gain_term, mlp_gain_term, norm_full, table_full), ('dp', '...  123 us
    reduce_scatter x1, waiting for transfers between devices, local(): lax.psum_scatter(jnp.einsum('tf,df->td', piece, w_glu, preferred_element_...  79.2 us
    reduce_scatter x1, waiting for transfers between devices, local(): lax.psum_scatter(jnp.concatenate([mix_part, glu_part], axis=1).astype(jnp...  72.7 us
    all_gather x1, waiting for transfers between devices, local(): input_all = lax.all_gather(block_input, 'mp', axis=0, tiled=True)  66.8 us
    all_gather x1, waiting for transfers between devices, local(): lax.all_gather(grad_middle.astype(jnp.bfloat16), 'mp', axis=0, tiled=True)  56.4 us
  transfers between devices with their start and end apart: 11, of which 9 were waited for; matrix products, arithmetic and copies ran while one was open for 23% of the time, Pallas kernels for 0%

commit v1 on v0

--- a/solution.py
+++ b/solution.py
@@ -10,6 +10,17 @@
 NDOM = 8
 EPS = 1e-06
 HIGH = lax.Precision.HIGHEST
+
+
+def pass_along(block, name, d):
+    count = lax.axis_size(name)
+    route = [(i, (i + 1) % count) for i in range(count)]
+    terms = [block]
+    for reach in range(1, count):
+        terms = [lax.ppermute(terms[0], name, route), *terms]
+    whole = jnp.concatenate(terms, axis=d)
+    shift = (lax.axis_index(name) + 1) * terms[-1].shape[d]
+    return jnp.roll(whole, shift, axis=d)
 
 
 def inverse_rms(rows):
@@ -147,7 +158,7 @@
     domain_hit = (domain_tags[:, None] == jnp.arange(NDOM)[None, :]).astype(jnp.float32)
     seq_count = jnp.dot(domain_hit, counts.astype(jnp.float32)[:, None], precision=HIGH)[:, 0]
     seq_weight = lax.rsqrt(seq_count)
-    cot_all = lax.all_gather(out_cotangent, "mp", axis=0, tiled=True)
+    cot_all = pass_along(out_cotangent, "mp", 0)
     grad_all = (
         cot_all.astype(jnp.float32).reshape(seqs, LEN, width) * seq_weight[:, None, None]
     ).reshape(total_rows, width)

time: 1440 us -> 1430 us (level)
  waiting for transfers between devices: 697 us -> 644 us
  starting transfers between devices: 0.85 us -> 30.3 us
  local copies, waits for them, and re-layouts: 78.9 us -> 101 us
    ppermute x0 -> x7, waiting for transfers between devices: none -> 87.9 us  [pass_along(): terms = [lax.ppermute(terms[0], name, route), *terms]]
    all_gather x1, waiting for transfers between devices: 66.8 us -> 0.01 us  [local(): input_all = lax.all_gather(block_input, 'mp', axis=0, tiled=True)]
    all_gather x1 -> x0, waiting for transfers between devices: 56.1 us -> none  [local(): cot_all = lax.all_gather(out_cotangent, 'mp', axis=0, tiled=True)]
    ppermute x0 -> x7, starting transfers between devices: none -> 29.5 us  [pass_along(): terms = [lax.ppermute(terms[0], name, route), *terms]]
    unnamed x91 -> x126, local copies, waits for them, and re-layouts: 25 us -> 45.6 us
    psum x1, waiting for transfers between devices: 146 us -> 127 us  [local(): lax.psum(partial_mix.astype(jnp.bfloat16), 'mp').astype(jnp.float32)]
  transfers between devices with their start and end apart: 11 -> 17, of which waited for: 9 -> 13; matrix products, arithmetic and copies ran while one was open for 23% -> 42% of each run, Pallas kernels for 0% -> 0%
where the time goes in v1:
time: 1430 us; the launch traced here: 1420 us
  waiting for transfers between devices  644 us (45%)
  matrix products  460 us (32%)
  local copies, waits for them, and re-layouts  101 us (7%)
  other arithmetic  86.2 us (6%)
  blocking collectives  79 us (6%)
  starting transfers between devices  30.3 us (2%)
  between operations  16.5 us (1%)
    dot_general x8, matrix products, forward_step(): jnp.einsum('cstu,csu->cst', weight, update_blk, precision=HIGH)  228 us
    dot_general x8, matrix products, backward_step(): jnp.einsum('cstu,cst->csu', weight, grad_blk, precision=HIGH)  142 us
    psum x1, waiting for transfers between devices, local(): lax.psum(partial_mix.astype(jnp.bfloat16), 'mp').astype(jnp.float32)  127 us
    psum x1, waiting for transfers between devices, local(): lax.psum((attn_gain_term, mlp_gain_term, norm_full, table_full), ('dp', '...  123 us
    ppermute x7, waiting for transfers between devices, pass_along(): terms = [lax.ppermute(terms[0], name, route), *terms]  87.9 us
    reduce_scatter x1, waiting for transfers between devices, local(): lax.psum_scatter(jnp.einsum('tf,df->td', piece, w_glu, preferred_element_...  81 us
    reduce_scatter x1, waiting for transfers between devices, local(): lax.psum_scatter(jnp.concatenate([mix_part, glu_part], axis=1).astype(jnp...  72.9 us
    all_gather x1, waiting for transfers between devices, local(): lax.all_gather(grad_middle.astype(jnp.bfloat16), 'mp', axis=0, tiled=True)  56.4 us
  transfers between devices with their start and end apart: 17, of which 13 were waited for; matrix products, arithmetic and copies ran while one was open for 42% of the time, Pallas kernels for 0%

profile of v1, /device:TPU:10, one launch (start us, length us, event | category | flops | bytes accessed | tf_op | source)
XLA Modules:
  0.0 1419.4 jit_solution(4213988494896739398)
XLA Ops:
  25.6 24.7 %collective-permute-done.1 = bf16[128,2048]{1,0:T(8,128)(2,1)S(1)} collective-permute-done((bf16[128,2048]{1,0:T(8,128)(2,1)S(1)}, bf16[128,2048]{1,0:T(8,128)(2,1)S(1)}, u32[]{:S(2)}, u32[]{:S(2)}) %collective-permute-start.1) | collective-permute-done | bytes 524320 | tf_op jit(solution)/shard_map/ppermute | solution.py:20
  52.2 18.4 %collective-permute-done.2 = bf16[128,2048]{1,0:T(8,128)(2,1)} collective-permute-done((bf16[128,2048]{1,0:T(8,128)(2,1)S(1)}, bf16[128,2048]{1,0:T(8,128)(2,1)}, u32[]{:S(2)}, u32[]{:S(2)}) %collective-permute-start.2) | collective-permute-done | bytes 524320 | tf_op jit(solution)/shard_map/ppermute | solution.py:20
  153.5 249.9 %while.32 = (s32[]{:T(128)}, f32[256,1]{0,1:T(1,128)S(1)}, f32[8,256,1,128]{1,3,2,0:T(8,128)}, f32[8,1,128]{2,1,0:T(1,128)S(1)}, f32[8,256,1,128]{3,2,1,0:T(1,128)}, /*index=5*/f32[8,256,1,128]{3,2,1,0:T(1,128)}, s32[]{:T(128)}) while((s32[]{:T(128)}, f32[256,1]{0,1:T(1,128)S(1)}, f32[8,256,1,128]{1,3,2,0:T(8,128)}, ...), condition=%wide.region_5.6_spmd.clone.clone, body=%wide.region_4.0_spmd.clone.clone.sunk | while | flops 113787008 | bytes 2398181 | solution.py:127
  155.4 28.5 %fusion.139 = f32[256,1,128]{2,1,0:T(1,128)S(1)} fusion(f32[256,128]{1,0:T(8,128)S(1)} %copy.93, pred[128,128]{1,0:T(8,128)(4,1)S(1)} %fusion.138, f32[8,256,1,128]{3,2,1,0:T(1,128)} %get-tuple-element.526, s32[]{:T(128)S(6)} %copy.104), kind=kOutput, calls=%fused_computation.2.clone.1 | convolution fusion | flops 62914560 | bytes 540676 | tf_op jit(solution)/shard_map/while/body/eval_jaxpr/cstu,csu->cst/dot_general | solution.py:122
  186.5 28.5 %fusion.139 = f32[256,1,128]{2,1,0:T(1,128)S(1)} fusion(f32[256,128]{1,0:T(8,128)S(1)} %copy.93, pred[128,128]{1,0:T(8,128)(4,1)S(1)} %fusion.138, f32[8,256,1,128]{3,2,1,0:T(1,128)} %get-tuple-element.526, s32[]{:T(128)S(6)} %copy.104), kind=kOutput, calls=%fused_computation.2.clone.1 | convolution fusion | flops 62914560 | bytes 540676 | tf_op jit(solution)/shard_map/while/body/eval_jaxpr/cstu,csu->cst/dot_general | solution.py:122
  217.7 28.5 %fusion.139 = f32[256,1,128]{2,1,0:T(1,128)S(1)} fusion(f32[256,128]{1,0:T(8,128)S(1)} %copy.93, pred[128,128]{1,0:T(8,128)(4,1)S(1)} %fusion.138, f32[8,256,1,128]{3,2,1,0:T(1,128)} %get-tuple-element.526, s32[]{:T(128)S(6)} %copy.104), kind=kOutput, calls=%fused_computation.2.clone.1 | convolution fusion | flops 62914560 | bytes 540676 | tf_op jit(solution)/shard_map/while/body/eval_jaxpr/cstu,csu->cst/dot_general | solution.py:122
  248.8 28.5 %fusion.139 = f32[256,1,128]{2,1,0:T(1,128)S(1)} fusion(f32[256,128]{1,0:T(8,128)S(1)} %copy.93, pred[128,128]{1,0:T(8,128)(4,1)S(1)} %fusion.138, f32[8,256,1,128]{3,2,1,0:T(1,128)} %get-tuple-element.526, s32[]{:T(128)S(6)} %copy.104), kind=kOutput, calls=%fused_computation.2.clone.1 | convolution fusion | flops 62914560 | bytes 540676 | tf_op jit(solution)/shard_map/while/body/eval_jaxpr/cstu,csu->cst/dot_general | solution.py:122
  280.0 28.5 %fusion.139 = f32[256,1,128]{2,1,0:T(1,128)S(1)} fusion(f32[256,128]{1,0:T(8,128)S(1)} %copy.93, pred[128,128]{1,0:T(8,128)(4,1)S(1)} %fusion.138, f32[8,256,1,128]{3,2,1,0:T(1,128)} %get-tuple-element.526, s32[]{:T(128)S(6)} %copy.104), kind=kOutput, calls=%fused_computation.2.clone.1 | convolution fusion | flops 62914560 | bytes 540676 | tf_op jit(solution)/shard_map/while/body/eval_jaxpr/cstu,csu->cst/dot_general | solution.py:122
  311.1 28.5 %fusion.139 = f32[256,1,128]{2,1,0:T(1,128)S(1)} fusion(f32[256,128]{1,0:T(8,128)S(1)} %copy.93, pred[128,128]{1,0:T(8,128)(4,1)S(1)} %fusion.138, f32[8,256,1,128]{3,2,1,0:T(1,128)} %get-tuple-element.526, s32[]{:T(128)S(6)} %copy.104), kind=kOutput, calls=%fused_computation.2.clone.1 | convolution fusion | flops 62914560 | bytes 540676 | tf_op jit(solution)/shard_map/while/body/eval_jaxpr/cstu,csu->cst/dot_general | solution.py:122
  342.3 28.5 %fusion.139 = f32[256,1,128]{2,1,0:T(1,128)S(1)} fusion(f32[256,128]{1,0:T(8,128)S(1)} %copy.93, pred[128,128]{1,0:T(8,128)(4,1)S(1)} %fusion.138, f32[8,256,1,128]{3,2,1,0:T(1,128)} %get-tuple-element.526, s32[]{:T(128)S(6)} %copy.104), kind=kOutput, calls=%fused_computation.2.clone.1 | convolution fusion | flops 62914560 | bytes 540676 | tf_op jit(solution)/shard_map/while/body/eval_jaxpr/cstu,csu->cst/dot_general | solution.py:122
  373.4 28.5 %fusion.139 = f32[256,1,128]{2,1,0:T(1,128)S(1)} fusion(f32[256,128]{1,0:T(8,128)S(1)} %copy.93, pred[128,128]{1,0:T(8,128)(4,1)S(1)} %fusion.138, f32[8,256,1,128]{3,2,1,0:T(1,128)} %get-tuple-element.526, s32[]{:T(128)S(6)} %copy.104), kind=kOutput, calls=%fused_computation.2.clone.1 | convolution fusion | flops 62914560 | bytes 540676 | tf_op jit(solution)/shard_map/while/body/eval_jaxpr/cstu,csu->cst/dot_general | solution.py:122
  407.4 19.9 %psum.49 = f32[1024]{0:T(1024)S(1)} all-reduce(f32[1024]{0:T(1024)S(1)} %bitcast.248), channel_id=1, replica_groups=mesh['dp'=4,'mp'=8] {'mp'}, use_global_device_ids=true, to_apply=%region_7.8 | all-reduce | flops 1024 | bytes 8192 | tf_op jit(solution)/shard_map/psum | solution.py:134
  461.2 127.2 %all-reduce.5.cloned.1.call-done = bf16[1024,2048]{1,0:T(8,128)(2,1)} async-done(((bf16[1024,2048]{1,0:T(8,128)(2,1)}), bf16[1024,2048]{1,0:T(8,128)(2,1)}) %all-reduce.5.cloned.1.call-update) | async-done | bytes 4194320 | tf_op jit(solution)/shard_map/psum | solution.py:140
  632.4 81.0 %reduce-scatter.9.cloned.1.call-done = bf16[128,2048]{1,0:T(8,128)(2,1)} async-done(((bf16[1024,2048]{1,0:T(8,128)(2,1)}), bf16[128,2048]{1,0:T(8,128)(2,1)}) %reduce-scatter.9.cloned.1.call-update) | async-done | bytes 524304 | tf_op jit(solution)/shard_map/reduce_scatter | solution.py:175
  734.1 56.4 %all-gather.5.cloned.1.call-done = bf16[1024,2048]{1,0:T(8,128)(2,1)} async-done(((bf16[128,2048]{1,0:T(8,128)(2,1)}), bf16[1024,2048]{1,0:T(8,128)(2,1)}) %all-gather.5.cloned.1.call-update) | async-done | bytes 4194320 | tf_op jit(solution)/shard_map/all_gather | solution.py:185
  821.7 182.9 %while.33 = (s32[]{:T(128)}, f32[256,1]{0,1:T(1,128)S(1)}, f32[8,256,1,128]{1,3,2,0:T(8,128)}, f32[8,256,1]{1,2,0:T(1,128)S(1)}, f32[8,1]{0,1:T(1,128)S(1)}, /*i...) while((s32[]{:T(128)}, f32[256,1]{0,1:T(1,128)S(1)}, ...), condition=%wide.region_18.19_spmd.clone.clone, body=%wide.region_17.18_spmd.clone.clone.sunk | while | flops 113853312 | bytes 2405947 | solution.py:208
  824.8 17.7 %fusion.150 = f32[256,1,128]{2,1,0:T(1,128)S(1)} fusion(f32[256,128]{1,0:T(8,128)S(1)} %copy.95, pred[128,128]{1,0:T(8,128)(4,1)S(1)} %fusion.149, f32[8,256,1,128]{3,2,1,0:T(1,128)} %get-tuple-element.557, s32[]{:T(128)S(6)} %sub.285), kind=kOutput, calls=%fused_computation.30.clone.1 | convolution fusion | flops 62914560 | bytes 540676 | tf_op jit(solution)/shard_map/while/body/eval_jaxpr/cstu,cst->csu/dot_general | solution.py:203
  847.6 17.7 %fusion.150 = f32[256,1,128]{2,1,0:T(1,128)S(1)} fusion(f32[256,128]{1,0:T(8,128)S(1)} %copy.95, pred[128,128]{1,0:T(8,128)(4,1)S(1)} %fusion.149, f32[8,256,1,128]{3,2,1,0:T(1,128)} %get-tuple-element.557, s32[]{:T(128)S(6)} %sub.285), kind=kOutput, calls=%fused_computation.30.clone.1 | convolution fusion | flops 62914560 | bytes 540676 | tf_op jit(solution)/shard_map/while/body/eval_jaxpr/cstu,cst->csu/dot_general | solution.py:203
  870.4 17.7 %fusion.150 = f32[256,1,128]{2,1,0:T(1,128)S(1)} fusion(f32[256,128]{1,0:T(8,128)S(1)} %copy.95, pred[128,128]{1,0:T(8,128)(4,1)S(1)} %fusion.149, f32[8,256,1,128]{3,2,1,0:T(1,128)} %get-tuple-element.557, s32[]{:T(128)S(6)} %sub.285), kind=kOutput, calls=%fused_computation.30.clone.1 | convolution fusion | flops 62914560 | bytes 540676 | tf_op jit(solution)/shard_map/while/body/eval_jaxpr/cstu,cst->csu/dot_general | solution.py:203
  1062.6 46.3 %reduce-scatter.11.cloned.1.call-done = bf16[128,2048]{1,0:T(8,128)(2,1)} async-done(((bf16[1024,2048]{1,0:T(8,128)(2,1)}), bf16[128,2048]{1,0:T(8,128)(2,1)}) %reduce-scatter.11.cloned.1.call-update) | async-done | bytes 524304 | tf_op jit(solution)/shard_map/reduce_scatter | solution.py:233
  1110.3 42.5 %all-reduce.1 = (f32[2048]{0:T(1024)}, f32[2048]{0:T(1024)}, f32[2048]{0:T(1024)}) all-reduce(f32[2048]{0:T(1024)S(1)} %get-tuple-element.358, f32[2048]{0:T(1024)S(1)} %get-tuple-element.354, f32[2048]{0:T(1024)S(1)} %mul.520), channel_id=1, replica_groups=mesh['dp'=4,'mp'=8] {'dp','mp'}, use_global_device_ids=true, to_apply=%region_22.23 | all-reduce | flops 6144 | bytes 49152 | tf_op jit(solution)/shard_map/psum | solution.py:265
  1152.8 48.6 %reduce-scatter.7.cloned.1.call-done = bf16[128,2048]{1,0:T(8,128)(2,1)} async-done(((bf16[1024,2048]{1,0:T(8,128)(2,1)}), bf16[128,2048]{1,0:T(8,128)(2,1)}) %reduce-scatter.7.cloned.1.call-update) | async-done | bytes 524304 | tf_op jit(solution)/shard_map/reduce_scatter | solution.py:151
  1205.0 72.9 %reduce-scatter.13.cloned.1.call-done = bf16[512,2176]{0,1:T(8,128)(2,1)} async-done(((bf16[2048,2176]{0,1:T(8,128)(2,1)}), bf16[512,2176]{0,1:T(8,128)(2,1)}) %reduce-scatter.13.cloned.1.call-update) | async-done | bytes 2228240 | tf_op jit(solution)/shard_map/reduce_scatter | solution.py:247
  1287.6 123.0 %all-reduce.7.cloned.1.call-done = f32[24,2048]{1,0:T(8,128)} async-done(((f32[24,2048]{1,0:T(8,128)}), f32[24,2048]{1,0:T(8,128)}) %all-reduce.7.cloned.1.call-update) | async-done | bytes 196624 | tf_op jit(solution)/shard_map/psum | solution.py:265
  (422 shorter events, 458.6 us)
Async XLA Ops:
  7.2 599.3 %copy-start = (bf16[704,2048]{1,0:T(8,128)(2,1)S(1)}, bf16[704,2048]{1,0:T(8,128)(2,1)}, u32[]{:S(2)}) copy-start(bf16[704,2048]{1,0:T(8,128)(2,1)} %param.35) | copy-start | bytes 8650756
  7.2 130.3 %all-gather.3.cloned.1.call-start = ((), (), s32[]{:S(2)}) async-start(), calls=%async_computation.6 | async-start | bytes 4718592 | tf_op jit(solution)/shard_map/all_gather | solution.py:79
  7.9 580.5 %all-reduce.5.cloned.1.call-start = ((), (), s32[]{:S(2)}) async-start(), calls=%async_computation.7 | async-start | bytes 8388608 | tf_op jit(solution)/shard_map/psum | solution.py:140
  8.0 15.6 %collective-permute-start = (bf16[128,2048]{1,0:T(8,128)(2,1)}, bf16[128,2048]{1,0:T(8,128)(2,1)S(1)}, u32[]{:S(2)}, u32[]{:S(2)}) collective-permute-start(bf16[128,2048]{1,0:T(8,128)(2,1)} %param.21), channel_id=1, source_target_pairs={{0,1},{1,2},{2,3},{3,4},{4,5},{5,6},{6,7},{7,0},{8,9},{9,10},{10,1... | collective-permute-start | bytes 1572872 | tf_op jit(solution)/shard_map/ppermute | solution.py:20
  24.3 26.0 %collective-permute-start.1 = (bf16[128,2048]{1,0:T(8,128)(2,1)S(1)}, bf16[128,2048]{1,0:T(8,128)(2,1)S(1)}, u32[]{:S(2)}, u32[]{:S(2)}) collective-permute-start(bf16[128,2048]{1,0:T(8,128)(2,1)S(1)} %collective-permute-done), channel_id=1, source_target_pairs={{0,1},{1,2},{2,3},{3,4},{4,5},{5,6},{6,7},{7,0},{8,9},{9,10},{10,1... | collective-permute-start | bytes 1572872 | tf_op jit(solution)/shard_map/ppermute | solution.py:20
  50.3 77.3 %copy-start.13 = (bf16[128,2048]{1,0:T(8,128)(2,1)}, bf16[128,2048]{1,0:T(8,128)(2,1)S(1)}, u32[]{:S(2)}) copy-start(bf16[128,2048]{1,0:T(8,128)(2,1)S(1)} %collective-permute-done.1) | copy-start | bytes 1572868
  50.3 20.3 %collective-permute-start.2 = (bf16[128,2048]{1,0:T(8,128)(2,1)S(1)}, bf16[128,2048]{1,0:T(8,128)(2,1)}, u32[]{:S(2)}, u32[]{:S(2)}) collective-permute-start(bf16[128,2048]{1,0:T(8,128)(2,1)S(1)} %collective-permute-done.1), channel_id=1, source_target_pairs={{0,1},{1,2},{2,3},{3,4},{4,5},{5,6},{6,7},{7,0},{8,9},{9,10},{10,1... | collective-permute-start | bytes 1572872 | tf_op jit(solution)/shard_map/ppermute | solution.py:20
  51.3 70.4 %copy-start.28 = (f32[256]{0:T(256)}, f32[256]{0:T(256)S(1)}, u32[]{:S(2)}) copy-start(f32[256]{0:T(256)S(1)} %reduce_max.9) | copy-start | bytes 3076
  51.3 59.5 %copy-start.17 = (bf16[2048,256]{1,0:T(8,128)(2,1)S(1)}, bf16[2048,256]{1,0:T(8,128)(2,1)}, u32[]{:S(2)}) copy-start(bf16[2048,256]{1,0:T(8,128)(2,1)} %param.31) | copy-start | bytes 3145732
  52.2 71.7 %copy-start.34 = (f32[256]{0:T(256)}, f32[256]{0:T(256)S(1)}, u32[]{:S(2)}) copy-start(f32[256]{0:T(256)S(1)} %fusion.85) | copy-start | bytes 3076
  70.6 26.1 %collective-permute-start.3 = (bf16[128,2048]{1,0:T(8,128)(2,1)}, bf16[128,2048]{1,0:T(8,128)(2,1)S(1)}, u32[]{:S(2)}, u32[]{:S(2)}) collective-permute-start(bf16[128,2048]{1,0:T(8,128)(2,1)} %collective-permute-done.2), channel_id=1, source_target_pairs={{0,1},{1,2},{2,3},{3,4},{4,5},{5,6},{6,7},{7,0},{8,9},{9,10},{10,1... | collective-permute-start | bytes 1572872 | tf_op jit(solution)/shard_map/ppermute | solution.py:20
  97.5 24.1 %collective-permute-start.4 = (bf16[128,2048]{1,0:T(8,128)(2,1)S(1)}, bf16[128,2048]{1,0:T(8,128)(2,1)}, u32[]{:S(2)}, u32[]{:S(2)}) collective-permute-start(bf16[128,2048]{1,0:T(8,128)(2,1)S(1)} %collective-permute-done.3), channel_id=1, source_target_pairs={{0,1},{1,2},{2,3},{3,4},{4,5},{5,6},{6,7},{7,0},{8,9},{9,10},{10,1... | collective-permute-start | bytes 1572872 | tf_op jit(solution)/shard_map/ppermute | solution.py:20
  121.7 12.0 collective-permute-start.5
  133.6 305.4 %collective-permute-start.6 = (bf16[128,2048]{1,0:T(8,128)(2,1)}, bf16[128,2048]{1,0:T(8,128)(2,1)}, u32[]{:S(2)}, u32[]{:S(2)}) collective-permute-start(bf16[128,2048]{1,0:T(8,128)(2,1)} %collective-permute-done.5), channel_id=1, source_target_pairs={{0,1},{1,2},{2,3},{3,4},{4,5},{5,6},{6,7},{7,0},{8,9},{9,10},{10,1... | collective-permute-start | bytes 1572872 | tf_op jit(solution)/shard_map/ppermute | solution.py:20
  153.5 273.8 %copy-start.40 = (f32[256]{0:T(256)S(1)}, f32[256]{0:T(256)}, u32[]{:S(2)}) copy-start(f32[256]{0:T(256)} %param.27) | copy-start | bytes 3076
  433.7 279.6 %reduce-scatter.9.cloned.1.call-start = ((), (), s32[]{:S(2)}) async-start(), calls=%async_computation.9 | async-start | bytes 4718592 | tf_op jit(solution)/shard_map/reduce_scatter | solution.py:175
  461.2 135.4 %copy-start.25 = (f32[2048]{0:T(1024)S(1)}, f32[2048]{0:T(1024)}, u32[]{:S(2)}) copy-start(f32[2048]{0:T(1024)} %param.26) | copy-start | bytes 24580
  624.3 166.1 %all-gather.5.cloned.1.call-start = ((), (), s32[]{:S(2)}) async-start(), calls=%async_computation.10 | async-start | bytes 4718592 | tf_op jit(solution)/shard_map/all_gather | solution.py:185
  718.0 339.2 %reduce-scatter.17.cloned.1.call-start = ((), (), s32[]{:S(2)}) async-start(), calls=%async_computation.15 | async-start | bytes 3604480 | tf_op jit(solution)/shard_map/reduce_scatter | solution.py:257
  725.9 334.8 %reduce-scatter.15.cloned.1.call-start = ((), (), s32[]{:S(2)}) async-start(), calls=%async_computation.14 | async-start | bytes 1310720 | tf_op jit(solution)/shard_map/reduce_scatter | solution.py:254
  820.6 288.2 %reduce-scatter.11.cloned.1.call-start = ((), (), s32[]{:S(2)}) async-start(), calls=%async_computation.11 | async-start | bytes 4718592 | tf_op jit(solution)/shard_map/reduce_scatter | solution.py:233
  1020.5 180.9 %reduce-scatter.7.cloned.1.call-start = ((), (), s32[]{:S(2)}) async-start(), calls=%async_computation.8 | async-start | bytes 4718592 | tf_op jit(solution)/shard_map/reduce_scatter | solution.py:151
  1027.0 250.9 %reduce-scatter.13.cloned.1.call-start = ((), (), s32[]{:S(2)}) async-start(), calls=%async_computation.13 | async-start | bytes 11141120 | tf_op jit(solution)/shard_map/reduce_scatter | solution.py:247
  1056.0 354.5 %all-reduce.7.cloned.1.call-start = ((), (), s32[]{:S(2)}) async-start(), calls=%async_computation.12 | async-start | bytes 393216 | tf_op jit(solution)/shard_map/psum | solution.py:265
  (40 other events, 353.1 us)
Sparse Core Ops, SparseCore 0:
  10.2 103.9 all-gather.2
  433.9 154.5 all-reduce.4
  624.5 88.8 reduce-scatter.8
  718.1 72.2 all-gather.4
  793.0 34.3 reduce-scatter.16
  829.7 24.8 reduce-scatter.14
  1020.6 88.2 reduce-scatter.10
  1112.5 88.8 reduce-scatter.6
  1204.2 73.6 reduce-scatter.12
  1284.8 125.7 all-reduce.6
